TPU v7x, 32 devices: a whole 2x2x4 slice. The times are simulated.
32 devices in a mesh: dp: 4 (over x, core), shard: 8 (over z, y).
Axes of the slice: x: 2, y: 2, z: 4, core: 2. Of those that a mesh axis runs over, the one named last changes fastest.
Arguments:
- tokens: bfloat16 [256, 6144], P('dp', 'shard'), may hold values from -6 to 6
- cotangent: bfloat16 [256, 6144], P('dp', 'shard'), may hold values from -12 to 12
- gate_proj: bfloat16 [2, 6144, 16384], P(None, 'dp', 'shard'), may hold values from -0.078125 to 0.078125
- up_proj: bfloat16 [2, 6144, 16384], P(None, 'dp', 'shard'), may hold values from -0.078125 to 0.078125
- down_proj: bfloat16 [2, 16384, 6144], P(None, 'shard', 'dp'), may hold values from -0.046875 to 0.046875
- slot_tokens: int32 [2, 64], P(None, 'dp'), may hold values from 0 to 63, as said below
- gate_weights: float32 [2, 64], P(None, 'dp'), may hold values from 0.1 to 1
- live_counts: int32 [2, 4], P(None, 'dp'), may hold values from 1 to 16, as said below
Outputs:
- grad_tokens: bfloat16 [256, 6144], P('dp', 'shard')
- grad_gate_proj: bfloat16 [2, 6144, 16384], P(None, 'dp', 'shard')
- grad_up_proj: bfloat16 [2, 6144, 16384], P(None, 'dp', 'shard')
- grad_down_proj: bfloat16 [2, 16384, 6144], P(None, 'shard', 'dp')
Inputs may be any that keep to these rules, and one draw needn't show every extreme that they name: `slot_tokens`: for each expert and each index of dp, the 16 slots name 16 different tokens of that index. `live_counts`: the live slots of an expert at an index of dp are its first ones; 16 is reached at some index of every expert.
All inputs are finite; a program needn't handle non-finite values.
Results may differ from a plain program's by a relative error of at most 0.03.
Values may be sent and summed in bfloat16 or wider, within the bound.
A program may use at most 128 MiB of HBM per device.

v0:
```python
import jax
import jax.numpy as jnp
from jax import lax
from jax.sharding import PartitionSpec as P


def slope_terms(gate_sum, up_sum, cot_hidden):
    sigmoid_part = jax.nn.sigmoid(gate_sum)
    grad_gate = (
        cot_hidden * up_sum * sigmoid_part * (1.0 + gate_sum * (1.0 - sigmoid_part))
    ).astype(jnp.bfloat16)
    grad_up = (cot_hidden * gate_sum * sigmoid_part).astype(jnp.bfloat16)
    return (grad_gate, grad_up)


def on_device(
    tokens, cotangent, gate_proj, up_proj, down_proj, slot_tokens, gate_weights, live_counts
):
    experts_here = slot_tokens.shape[0]
    slot_count = slot_tokens.shape[1]
    token_count = tokens.shape[0]
    position = lax.broadcasted_iota(jnp.int32, slot_tokens.shape, 1)
    alive_mask = (position < live_counts).astype(jnp.float32)
    picked = tokens[slot_tokens]
    weighted = (
        cotangent[slot_tokens].astype(jnp.float32) * (gate_weights * alive_mask)[:, :, None]
    ).astype(jnp.bfloat16)
    full_rows, full_cot = (
        lax.all_gather(picked, "shard", axis=2, tiled=True),
        lax.all_gather(weighted, "shard", axis=2, tiled=True),
    )
    block_rows, block_cot = (
        lax.all_to_all(full_rows, "dp", split_axis=2, concat_axis=1, tiled=True),
        lax.all_to_all(full_cot, "dp", split_axis=2, concat_axis=1, tiled=True),
    )
    totals = lax.psum(live_counts, "dp").astype(jnp.float32)
    gate_part = jnp.einsum(
        "erd,edf->erf", block_rows, gate_proj, preferred_element_type=jnp.float32
    )
    up_part = jnp.einsum("erd,edf->erf", block_rows, up_proj, preferred_element_type=jnp.float32)
    cot_part = jnp.einsum("erd,efd->erf", block_cot, down_proj, preferred_element_type=jnp.float32)
    gate_total, up_total = (
        lax.psum(gate_part.astype(jnp.bfloat16), "dp").astype(jnp.float32),
        lax.psum(up_part.astype(jnp.bfloat16), "dp").astype(jnp.float32),
    )
    hidden_all = (jax.nn.silu(gate_total) * up_total).astype(jnp.bfloat16)
    cot_total = lax.psum(cot_part.astype(jnp.bfloat16), "dp").astype(jnp.float32)
    gate_all, up_all = slope_terms(gate_total, up_total, cot_total)
    scale_back = totals[:, :, None]
    grad_down_proj = (
        jnp.einsum("erf,erd->efd", hidden_all, block_cot, preferred_element_type=jnp.float32)
        / scale_back
    ).astype(jnp.bfloat16)
    grad_gate_proj = (
        jnp.einsum("erd,erf->edf", block_rows, gate_all, preferred_element_type=jnp.float32)
        / scale_back
    ).astype(jnp.bfloat16)
    grad_up_proj = (
        jnp.einsum("erd,erf->edf", block_rows, up_all, preferred_element_type=jnp.float32)
        / scale_back
    ).astype(jnp.bfloat16)
    back_term = (
        jnp.einsum("erf,edf->erd", gate_all, gate_proj, preferred_element_type=jnp.float32)
        + jnp.einsum("erf,edf->erd", up_all, up_proj, preferred_element_type=jnp.float32)
    ).astype(jnp.bfloat16)
    owned_rows = lax.all_to_all(back_term, "dp", split_axis=1, concat_axis=2, tiled=True)
    row_grads = lax.psum_scatter(
        owned_rows.astype(jnp.float32).astype(jnp.bfloat16),
        "shard",
        scatter_dimension=2,
        tiled=True,
    ).astype(jnp.float32)
    one_hot = (
        slot_tokens[:, :, None]
        == lax.broadcasted_iota(jnp.int32, (experts_here, slot_count, token_count), 2)
    ).astype(jnp.float32)
    grad_tokens = jnp.einsum("ert,erf->tf", one_hot, row_grads).astype(jnp.bfloat16)
    return (grad_tokens, grad_gate_proj, grad_up_proj, grad_down_proj)


def solution(mesh):
    in_specs = (
        P("dp", "shard"),
        P("dp", "shard"),
        P(None, "dp", "shard"),
        P(None, "dp", "shard"),
        P(None, "shard", "dp"),
        P(None, "dp"),
        P(None, "dp"),
        P(None, "dp"),
    )
    out_specs = (
        P("dp", "shard"),
        P(None, "dp", "shard"),
        P(None, "dp", "shard"),
        P(None, "shard", "dp"),
    )
    return jax.shard_map(
        on_device, mesh=mesh, in_specs=in_specs, out_specs=out_specs, check_vma=False
    )
```

profile of v0, /device:TPU:0, one launch (start us, length us, event | category | flops | bytes accessed | tf_op | source)
XLA Modules:
  0.0 307.7 jit_solution(18017264233754935161)
XLA Ops:
  7.2 0.0 copy-start
  7.2 0.7 compare_select_fusion
  7.9 0.1 reshape.13
  8.0 0.1 copy-done
  8.1 0.6 gather_fusion.1
  8.7 34.9 %all-gather = bf16[2,16,6144]{2,1,0:T(8,128)(2,1)} all-gather(bf16[2,16,768]{2,1,0:T(8,128)(2,1)S(1)} %bitcast.48), channel_id=2, replica_groups=mesh['dp'=4,'shard'=8] {'shard'}, dimensions={2}, use_global_device_ids=true | all-gather | bytes 442368 | tf_op jit(solution)/shard_map/all_gather | solution.py:29
  43.6 6.1 %copy.27 = bf16[2,16,6144]{1,0,2:T(2,128)(2,1)S(1)} copy(bf16[2,16,6144]{2,1,0:T(8,128)(2,1)} %all-gather) | data formatting | bytes 786432 | tf_op jit(solution)/shard_map/all_gather | solution.py:29
  49.7 3.9 %reshape.34 = bf16[4,2,24576]{2,1,0:T(2,128)(2,1)} reshape(bf16[6144,2,16]{2,1,0:T(2,128)(2,1)S(1)} %bitcast.39) | data formatting | bytes 786432
  53.6 4.1 %all-to-all-start.1 = ((bf16[4,2,24576]{2,1,0:T(2,128)(2,1)}), bf16[4,2,24576]{2,1,0:T(2,128)(2,1)}, u32[]{:S(2)}, u32[]{:S(2)}) async-start(bf16[4,2,24576]{2,1,0:T(2,128)(2,1)} %reshape.34), calls=%async_computation.1 | async-start | bytes 786432 | tf_op jit(solution)/shard_map/all_to_all | solution.py:33
  57.7 1.6 gather_fusion
  59.3 0.8 compare_select_fusion.1
  60.0 0.1 fusion.14
  60.1 33.0 %all_gather.6 = bf16[2,16,6144]{2,1,0:T(8,128)(2,1)} all-gather(bf16[2,16,768]{2,1,0:T(8,128)(2,1)S(1)} %fusion.14), channel_id=1, replica_groups=mesh['dp'=4,'shard'=8] {'shard'}, dimensions={2}, use_global_device_ids=true | all-gather | bytes 442368 | tf_op jit(solution)/shard_map/all_gather | solution.py:30
  93.1 6.1 %copy.24 = bf16[2,16,6144]{1,0,2:T(2,128)(2,1)S(1)} copy(bf16[2,16,6144]{2,1,0:T(8,128)(2,1)} %all_gather.6) | data formatting | bytes 786432 | tf_op jit(solution)/shard_map/all_gather | solution.py:30
  99.2 3.9 %reshape.36 = bf16[4,2,24576]{2,1,0:T(2,128)(2,1)} reshape(bf16[6144,2,16]{2,1,0:T(2,128)(2,1)S(1)} %bitcast.40) | data formatting | bytes 786432
  103.1 0.0 all-to-all-done.1
  103.1 4.1 %all-to-all-start = ((bf16[4,2,24576]{2,1,0:T(2,128)(2,1)}), bf16[4,2,24576]{2,1,0:T(2,128)(2,1)}, u32[]{:S(2)}, u32[]{:S(2)}) async-start(bf16[4,2,24576]{2,1,0:T(2,128)(2,1)} %reshape.36), calls=%async_computation | async-start | bytes 786432 | tf_op jit(solution)/shard_map/all_to_all | solution.py:34
  107.2 0.0 all-reduce.3.cloned.1.call-start
  107.2 3.5 %reshape.35 = bf16[6144,2,16]{2,1,0:T(2,128)(2,1)S(1)} reshape(bf16[4,2,24576]{2,1,0:T(2,128)(2,1)} %all-to-all-done.1) | data formatting | bytes 786432
  110.7 4.8 %copy.33 = bf16[2,16,4,1536]{3,2,1,0:T(4,128)(2,1)} copy(bf16[2,16,4,1536]{1,0,3,2:T(2,128)(2,1)S(1)} %bitcast.41) | data formatting | bytes 786432 | tf_op jit(solution)/shard_map/all_to_all | solution.py:33
  115.6 1.1 copy.29
  116.6 7.7 %convolution_convert_fusion = bf16[2,64,2048]{2,1,0:T(8,128)(2,1)} fusion(bf16[2,64,1536]{2,1,0:T(8,128)(2,1)S(1)} %bitcast.35, bf16[2,1536,2048]{2,1,0:T(8,128)(2,1)} %param.10), kind=kOutput, calls=%fused_computation.6 | convolution fusion | flops 805568512 | bytes 13500416 | tf_op jit(solution)/shard_map/erd,edf->erf/dot_general | solution.py:37
  124.3 7.7 %convolution_convert_fusion.1 = bf16[2,64,2048]{2,1,0:T(8,128)(2,1)} fusion(bf16[2,64,1536]{2,1,0:T(8,128)(2,1)S(1)} %bitcast.36, bf16[2,1536,2048]{2,1,0:T(8,128)(2,1)} %param.11), kind=kOutput, calls=%fused_computation.7 | convolution fusion | flops 805568512 | bytes 13500416 | tf_op jit(solution)/shard_map/erd,edf->erf/dot_general | solution.py:40
  132.0 0.0 copy-start.3
  132.0 0.0 all-to-all-done
  132.0 4.7 %reshape.37 = bf16[6144,2,16]{2,1,0:T(2,128)(2,1)} reshape(bf16[4,2,24576]{2,1,0:T(2,128)(2,1)} %all-to-all-done) | data formatting | bytes 786432
  136.7 7.3 %copy.32 = bf16[2,16,4,1536]{3,2,1,0:T(4,128)(2,1)S(1)} copy(bf16[2,16,4,1536]{1,0,3,2:T(2,128)(2,1)} %bitcast.42) | data formatting | bytes 786432 | tf_op jit(solution)/shard_map/all_to_all | solution.py:34
  144.0 0.1 copy.26
  144.0 9.2 %convolution_convert_fusion.2 = bf16[2,64,2048]{2,1,0:T(8,128)(2,1)} fusion(bf16[2,64,1536]{2,1,0:T(8,128)(2,1)S(1)} %bitcast.43, bf16[2,2048,1536]{2,1,0:T(8,128)(2,1)} %param.12), kind=kOutput, calls=%fused_computation.8 | convolution fusion | flops 805568512 | bytes 13500416 | tf_op jit(solution)/shard_map/erd,efd->erf/dot_general | solution.py:41
  153.3 0.0 all-reduce.3.cloned.1.call-update
  153.3 0.0 copy-done.3
  153.3 5.6 %psum.31 = s32[2,1]{0,1:T(1,128)S(1)} all-reduce(s32[2,1]{0,1:T(1,128)S(1)} %copy-done.3), channel_id=1, replica_groups=mesh['dp'=4,'shard'=8] {'dp'}, use_global_device_ids=true, to_apply=%region_4.5 | all-reduce | flops 2 | bytes 16 | tf_op jit(solution)/shard_map/psum | solution.py:36
  158.9 39.1 %all-reduce.3.cloned.1.call-done = (bf16[2,64,2048]{2,1,0:T(8,128)(2,1)}, bf16[2,64,2048]{2,1,0:T(8,128)(2,1)}, bf16[2,64,2048]{2,1,0:T(8,128)(2,1)}) async-done(((bf16[2,64,2048]{2,1,0:T(8,128)(2,1)}, bf16[2,64,2048]{2,1,0:T(8,128)(2,1)}, bf16[2,64,2048]{2,1,0:T(8,128)(2,1)}), (bf16[2,64,2048]{2,1,0:T(8,128)(2,1)}, bf16[2,64,2048]{2,1,0:T(8,128)(2,1)}, ...) | async-done | bytes 1572880 | tf_op jit(solution)/shard_map/psum | solution.py:44
  198.0 0.0 copy-start.4
  198.0 0.0 copy-start.5
  198.0 9.1 %fusion.20 = f32[2,64,1536]{2,1,0:T(8,128)S(1)} fusion(bf16[2,1536,2048]{2,1,0:T(8,128)(2,1)} %param.10, bf16[2,64,2048]{2,1,0:T(8,128)(2,1)} %get-tuple-element.4, bf16[2,64,2048]{2,1,0:T(8,128)(2,1)} %get-tuple-element.5, bf16[2,64,2048]{2,1,0:T(8,128)(2,1)} %get-tuple-element.6), kind=kOutput, calls=%fused_computation.38 | convolution fusion | flops 808714240 | bytes 14942208 | tf_op jit(solution)/shard_map/erf,edf->erd/dot_general | solution.py:63
  207.1 0.0 copy-done.4
  207.1 0.0 copy-done.5
  207.1 0.0 copy-start.6
  207.1 8.6 %fusion = bf16[2,64,1536]{2,1,0:T(8,128)(2,1)S(1)} fusion(f32[2,64,1536]{2,1,0:T(8,128)S(1)} %fusion.20, bf16[2,1536,2048]{2,1,0:T(8,128)(2,1)} %param.11, bf16[2,64,2048]{2,1,0:T(8,128)(2,1)S(1)} %copy-done.5, bf16[2,64,2048]{2,1,0:T(8,128)(2,1)S(1)} %copy-done.4), kind=kOutput, calls=%fused_computation.9 | convolution fusion | flops 807796736 | bytes 14811136 | tf_op jit(solution)/shard_map/erf,edf->erd/dot_general | solution.py:64
  215.7 1.2 copy.30
  216.8 3.5 %all-to-all-start.2 = ((bf16[2,64,1536]{2,0,1:T(2,128)(2,1)}), bf16[2,64,1536]{2,0,1:T(2,128)(2,1)S(1)}, u32[]{:S(2)}, u32[]{:S(2)}) async-start(bf16[2,64,1536]{2,0,1:T(2,128)(2,1)} %copy.30), calls=%async_computation.2 | async-start | bytes 786432 | tf_op jit(solution)/shard_map/all_to_all | solution.py:66
  220.3 0.3 reduce-scatter.2.cloned.1.call-start
  220.5 0.0 copy-done.6
  220.6 6.7 %divide_convert_fusion.2 = bf16[2,1536,2048]{2,1,0:T(8,128)(2,1)} fusion(f32[2]{0:T(128)S(1)} %convert_bitcast_fusion, bf16[2,64,1536]{2,1,0:T(8,128)(2,1)S(1)} %bitcast.37, bf16[2,64,2048]{2,1,0:T(8,128)(2,1)S(1)} %copy-done.6, bf16[2,64,2048]{2,1,0:T(8,128)(2,1)S(1)} %copy-done.4, bf16[2,64,2048]{2,1,0:T(8,128)(2,1)S(1)} %copy-done.5), kind=kOutput, calls=%fused_computation.4 | convolution fusion | flops 821297152 | bytes 14549000 | tf_op jit(solution)/shard_map/erd,erf->edf/dot_general | solution.py:55
  227.3 6.9 %divide_convert_fusion = bf16[2,2048,1536]{2,1,0:T(8,128)(2,1)} fusion(f32[2]{0:T(128)S(1)} %convert_bitcast_fusion, bf16[2,64,1536]{2,1,0:T(8,128)(2,1)S(1)} %bitcast.44, bf16[2,64,2048]{2,1,0:T(8,128)(2,1)S(1)} %copy-done.6, bf16[2,64,2048]{2,1,0:T(8,128)(2,1)S(1)} %copy-done.5), kind=kOutput, calls=%fused_computation.2 | convolution fusion | flops 819986432 | bytes 14024712 | tf_op jit(solution)/shard_map/erf,erd->efd/dot_general | solution.py:51
  234.2 0.0 all-to-all-done.2
  234.2 0.3 copy.31
  234.5 1.0 all_to_all.50
  235.5 0.0 reduce-scatter.2.cloned.1.call-update
  235.5 0.0 copy-start.2
  235.5 0.0 copy-start.1
  235.6 6.7 %divide_convert_fusion.1 = bf16[2,1536,2048]{2,1,0:T(8,128)(2,1)} fusion(f32[2]{0:T(128)S(1)} %convert_bitcast_fusion, bf16[2,64,1536]{2,1,0:T(8,128)(2,1)S(1)} %bitcast.38, bf16[2,64,2048]{2,1,0:T(8,128)(2,1)S(1)} %copy-done.5, bf16[2,64,2048]{2,1,0:T(8,128)(2,1)S(1)} %copy-done.4), kind=kOutput, calls=%fused_computation.3 | convolution fusion | flops 819986432 | bytes 14024712 | tf_op jit(solution)/shard_map/erd,erf->edf/dot_general | solution.py:59
  242.3 56.8 %reduce-scatter.2.cloned.1.call-done = bf16[2,16,768]{2,1,0:T(8,128)(2,1)} async-done(((bf16[2,16,6144]{2,1,0:T(8,128)(2,1)}), bf16[2,16,768]{2,1,0:T(8,128)(2,1)}) %reduce-scatter.2.cloned.1.call-update) | async-done | bytes 49168 | tf_op jit(solution)/shard_map/reduce_scatter | solution.py:67
  299.1 0.0 copy-done.2
  299.1 1.7 fusion.1
  300.8 0.0 copy-done.1
  (2 shorter events, 0.0 us)
Async XLA Ops:
  7.2 0.9 copy-start
  53.6 49.5 %all-to-all-start.1 = ((bf16[4,2,24576]{2,1,0:T(2,128)(2,1)}), bf16[4,2,24576]{2,1,0:T(2,128)(2,1)}, u32[]{:S(2)}, u32[]{:S(2)}) async-start(bf16[4,2,24576]{2,1,0:T(2,128)(2,1)} %reshape.34), calls=%async_computation.1 | async-start | bytes 786432 | tf_op jit(solution)/shard_map/all_to_all | solution.py:33
  103.1 28.9 %all-to-all-start = ((bf16[4,2,24576]{2,1,0:T(2,128)(2,1)}), bf16[4,2,24576]{2,1,0:T(2,128)(2,1)}, u32[]{:S(2)}, u32[]{:S(2)}) async-start(bf16[4,2,24576]{2,1,0:T(2,128)(2,1)} %reshape.36), calls=%async_computation | async-start | bytes 786432 | tf_op jit(solution)/shard_map/all_to_all | solution.py:34
  107.2 90.8 %all-reduce.3.cloned.1.call-start = ((), (), s32[]{:S(2)}) async-start(), calls=%async_computation.5 | async-start | bytes 3145728 | tf_op jit(solution)/shard_map/psum | solution.py:44
  132.0 21.3 %copy-start.3 = (s32[2,1]{0,1:T(1,128)S(1)}, s32[2,1]{0,1:T(1,128)}, u32[]{:S(2)}) copy-start(s32[2,1]{0,1:T(1,128)} %param.15) | copy-start | bytes 28
  198.0 9.1 %copy-start.4 = (bf16[2,64,2048]{2,1,0:T(8,128)(2,1)S(1)}, bf16[2,64,2048]{2,1,0:T(8,128)(2,1)}, u32[]{:S(2)}) copy-start(bf16[2,64,2048]{2,1,0:T(8,128)(2,1)} %get-tuple-element.5) | copy-start | bytes 1572868
  198.0 9.1 %copy-start.5 = (bf16[2,64,2048]{2,1,0:T(8,128)(2,1)S(1)}, bf16[2,64,2048]{2,1,0:T(8,128)(2,1)}, u32[]{:S(2)}) copy-start(bf16[2,64,2048]{2,1,0:T(8,128)(2,1)} %get-tuple-element.6) | copy-start | bytes 1572868
  207.1 13.5 %copy-start.6 = (bf16[2,64,2048]{2,1,0:T(8,128)(2,1)S(1)}, bf16[2,64,2048]{2,1,0:T(8,128)(2,1)}, u32[]{:S(2)}) copy-start(bf16[2,64,2048]{2,1,0:T(8,128)(2,1)} %get-tuple-element.4) | copy-start | bytes 1572868
  216.8 17.4 %all-to-all-start.2 = ((bf16[2,64,1536]{2,0,1:T(2,128)(2,1)}), bf16[2,64,1536]{2,0,1:T(2,128)(2,1)S(1)}, u32[]{:S(2)}, u32[]{:S(2)}) async-start(bf16[2,64,1536]{2,0,1:T(2,128)(2,1)} %copy.30), calls=%async_computation.2 | async-start | bytes 786432 | tf_op jit(solution)/shard_map/all_to_all | solution.py:66
  220.3 78.8 %reduce-scatter.2.cloned.1.call-start = ((), (), s32[]{:S(2)}) async-start(), calls=%async_computation.4 | async-start | bytes 442368 | tf_op jit(solution)/shard_map/reduce_scatter | solution.py:67
  235.5 63.6 %copy-start.2 = (s32[2,16]{1,0:T(2,128)S(1)}, s32[2,16]{1,0:T(2,128)}, u32[]{:S(2)}) copy-start(s32[2,16]{1,0:T(2,128)} %param.13) | copy-start | bytes 388
  235.5 65.3 %copy-start.1 = (bf16[64,768]{1,0:T(8,128)(2,1)S(1)}, bf16[64,768]{1,0:T(8,128)(2,1)}, u32[]{:S(2)}) copy-start(bf16[64,768]{1,0:T(8,128)(2,1)} %param.8) | copy-start | bytes 294916
Sparse Core Ops, SparseCore 0:
  153.4 44.5 all-reduce.2
  235.7 63.4 reduce-scatter.1
where the time goes:
time: 309 us; the launch traced here: 308 us
  waiting for transfers between devices  96 us (31%)
  blocking collectives  73.4 us (24%)
  matrix products  64.3 us (21%)
  local copies, waits for them, and re-layouts  46.3 us (15%)
  between operations  14.2 us (5%)
  starting transfers between devices  12 us (4%)
    reduce_scatter x1, waiting for transfers between devices, on_device(): lax.psum_scatter(owned_rows.astype(jnp.float32).astype(jnp.bfloat16), 'sh...  56.8 us
    psum x1, waiting for transfers between devices, on_device(): lax.psum(up_part.astype(jnp.bfloat16), 'dp').astype(jnp.float32)  39.1 us
    all_gather x1, blocking collectives, on_device(): lax.all_gather(picked, 'shard', axis=2, tiled=True)  34.9 us
    all_gather x1, blocking collectives, on_device(): lax.all_gather(weighted, 'shard', axis=2, tiled=True)  33 us
    unnamed x18, local copies, waits for them, and re-layouts  16.1 us
    dot_general x1, matrix products, on_device(): jnp.einsum('erd,efd->erf', block_cot, down_proj, preferred_element_type=j...  9.24 us
    dot_general x1, matrix products, on_device(): jnp.einsum('erf,edf->erd', gate_all, gate_proj, preferred_element_type=jn...  9.06 us
    dot_general x1, matrix products, on_device(): jnp.einsum('erf,edf->erd', up_all, up_proj, preferred_element_type=jnp.fl...  8.55 us
  transfers between devices with their start and end apart: 5, of which 2 were waited for; matrix products, arithmetic and copies ran while one was open for 19% of the time, Pallas kernels for 0%

commit v1 on v0

--- a/solution.py
+++ b/solution.py
@@ -1,7 +1,16 @@
+import functools
 import jax
 import jax.numpy as jnp
 from jax import lax
 from jax.sharding import PartitionSpec as P
+
+
+def draft_outputs_up(vals, axis_tag):
+    y1 = jnp.concatenate(lax.all_gather(vals, axis_tag), 2)
+    return y1
+
+
+scan_run = functools.partial(draft_outputs_up, axis_tag="shard")
 
 
 def slope_terms(gate_sum, up_sum, cot_hidden):
@@ -25,10 +34,7 @@
     weighted = (
         cotangent[slot_tokens].astype(jnp.float32) * (gate_weights * alive_mask)[:, :, None]
     ).astype(jnp.bfloat16)
-    full_rows, full_cot = (
-        lax.all_gather(picked, "shard", axis=2, tiled=True),
-        lax.all_gather(weighted, "shard", axis=2, tiled=True),
-    )
+    full_rows, full_cot = (lax.all_gather(picked, "shard", axis=2, tiled=True), scan_run(weighted))
     block_rows, block_cot = (
         lax.all_to_all(full_rows, "dp", split_axis=2, concat_axis=1, tiled=True),
         lax.all_to_all(full_cot, "dp", split_axis=2, concat_axis=1, tiled=True),

time: 309 us -> 305 us (0.987)
  blocking collectives: 73.4 us -> 69.4 us
    all_gather x1 -> x0, local copies, waits for them, and re-layouts: 6.1 us -> none  [on_device(): lax.all_gather(weighted, 'shard', axis=2, tiled=True)]
    reshape x0 -> x1, local copies, waits for them, and re-layouts: none -> 5.43 us  [draft_outputs_up(): y1 = jnp.concatenate(lax.all_gather(vals, axis_tag), 2)]
  transfers between devices with their start and end apart: 5 -> 5, of which waited for: 2 -> 2; matrix products, arithmetic and copies ran while one was open for 19% -> 20% of each run, Pallas kernels for 0% -> 0%
where the time goes in v1:
time: 305 us; the launch traced here: 304 us
  waiting for transfers between devices  95.8 us (31%)
  blocking collectives  69.4 us (23%)
  matrix products  64.3 us (21%)
  local copies, waits for them, and re-layouts  47.7 us (16%)
  between operations  14.2 us (5%)
  starting transfers between devices  10.7 us (4%)
    reduce_scatter x1, waiting for transfers between devices, on_device(): lax.psum_scatter(owned_rows.astype(jnp.float32).astype(jnp.bfloat16), 'sh...  56.8 us
    psum x1, waiting for transfers between devices, on_device(): lax.psum(up_part.astype(jnp.bfloat16), 'dp').astype(jnp.float32)  38.9 us
    all_gather x1, blocking collectives, on_device(): lax.all_gather(picked, 'shard', axis=2, tiled=True)  32.8 us
    all_gather x1, blocking collectives, draft_outputs_up(): y1 = jnp.concatenate(lax.all_gather(vals, axis_tag), 2)  31 us
    unnamed x18, local copies, waits for them, and re-layouts  17.8 us
    dot_general x1, matrix products, on_device(): jnp.einsum('erd,efd->erf', block_cot, down_proj, preferred_element_type=j...  9.24 us
    dot_general x1, matrix products, on_device(): jnp.einsum('erf,edf->erd', gate_all, gate_proj, preferred_element_type=jn...  9.06 us
    dot_general x1, matrix products, on_device(): jnp.einsum('erf,edf->erd', up_all, up_proj, preferred_element_type=jnp.fl...  8.55 us
  transfers between devices with their start and end apart: 5, of which 2 were waited for; matrix products, arithmetic and copies ran while one was open for 20% of the time, Pallas kernels for 0%

profile of v1, /device:TPU:0, one launch (start us, length us, event | category | flops | bytes accessed | tf_op | source)
XLA Modules:
  0.0 303.6 jit_solution(1542758554800516065)
XLA Ops:
  7.2 0.0 copy-start
  7.2 0.7 compare_select_fusion
  7.9 0.1 reshape.37
  8.0 0.1 copy-done
  8.1 0.6 gather_fusion.1
  8.7 32.8 %all-gather = bf16[2,16,6144]{2,1,0:T(8,128)(2,1)S(1)} all-gather(bf16[2,16,768]{2,1,0:T(8,128)(2,1)S(1)} %bitcast.51), channel_id=2, replica_groups=mesh['dp'=4,'shard'=8] {'shard'}, dimensions={2}, use_global_device_ids=true | all-gather | bytes 442368 | tf_op jit(solution)/shard_map/all_gather | solution.py:37
  41.5 5.0 %copy.30 = bf16[2,16,6144]{1,0,2:T(2,128)(2,1)} copy(bf16[2,16,6144]{2,1,0:T(8,128)(2,1)S(1)} %all-gather) | data formatting | bytes 786432 | tf_op jit(solution)/shard_map/all_gather | solution.py:37
  46.5 5.4 %reshape.59 = bf16[4,2,24576]{2,1,0:T(2,128)(2,1)} reshape(bf16[6144,2,16]{2,1,0:T(2,128)(2,1)} %bitcast.41) | data formatting | bytes 786432
  51.9 3.5 %all-to-all-start.1 = ((bf16[4,2,24576]{2,1,0:T(2,128)(2,1)}), bf16[4,2,24576]{2,1,0:T(2,128)(2,1)S(1)}, u32[]{:S(2)}, u32[]{:S(2)}) async-start(bf16[4,2,24576]{2,1,0:T(2,128)(2,1)} %reshape.59), calls=%async_computation.1 | async-start | bytes 786432 | tf_op jit(solution)/shard_map/all_to_all | solution.py:39
  55.4 1.6 gather_fusion
  57.0 0.8 compare_select_fusion.1
  57.7 0.1 fusion.14
  57.8 31.0 %all_gather.7 = bf16[8,2,16,768]{3,2,1,0:T(8,128)(2,1)S(1)} all-gather(bf16[1,2,16,768]{3,2,1,0:T(8,128)(2,1)S(1)} %fusion.14), channel_id=1, replica_groups=mesh['dp'=4,'shard'=8] {'shard'}, dimensions={0}, use_global_device_ids=true | all-gather | bytes 442368 | tf_op jit(solution)/shard_map/all_gather | solution.py:9
  88.7 5.4 %copy.35 = bf16[2,16,8,768]{1,0,3,2:T(2,128)(2,1)} copy(bf16[2,16,8,768]{3,1,0,2:T(8,128)(2,1)S(1)} %bitcast.48) | data formatting | bytes 786432 | tf_op jit(solution)/shard_map/reshape | solution.py:9
  94.2 5.4 %reshape.61 = bf16[4,2,24576]{2,1,0:T(2,128)(2,1)} reshape(bf16[6144,2,16]{2,1,0:T(2,128)(2,1)} %bitcast.42) | data formatting | bytes 786432
  99.6 0.0 all-to-all-done.1
  99.6 3.5 %all-to-all-start = ((bf16[4,2,24576]{2,1,0:T(2,128)(2,1)}), bf16[4,2,24576]{2,1,0:T(2,128)(2,1)S(1)}, u32[]{:S(2)}, u32[]{:S(2)}) async-start(bf16[4,2,24576]{2,1,0:T(2,128)(2,1)} %reshape.61), calls=%async_computation | async-start | bytes 786432 | tf_op jit(solution)/shard_map/all_to_all | solution.py:40
  103.1 0.0 all-reduce.3.cloned.1.call-start
  103.1 3.4 %reshape.60 = bf16[6144,2,16]{2,1,0:T(2,128)(2,1)} reshape(bf16[4,2,24576]{2,1,0:T(2,128)(2,1)S(1)} %all-to-all-done.1) | data formatting | bytes 786432
  106.5 7.3 %copy.37 = bf16[2,16,4,1536]{3,2,1,0:T(4,128)(2,1)S(1)} copy(bf16[2,16,4,1536]{1,0,3,2:T(2,128)(2,1)} %bitcast.43) | data formatting | bytes 786432 | tf_op jit(solution)/shard_map/all_to_all | solution.py:39
  113.8 0.1 copy.32
  113.9 7.7 %convolution_convert_fusion = bf16[2,64,2048]{2,1,0:T(8,128)(2,1)} fusion(bf16[2,64,1536]{2,1,0:T(8,128)(2,1)S(1)} %bitcast.37, bf16[2,1536,2048]{2,1,0:T(8,128)(2,1)} %param.10), kind=kOutput, calls=%fused_computation.6 | convolution fusion | flops 805568512 | bytes 13500416 | tf_op jit(solution)/shard_map/erd,edf->erf/dot_general | solution.py:43
  121.6 7.7 %convolution_convert_fusion.1 = bf16[2,64,2048]{2,1,0:T(8,128)(2,1)} fusion(bf16[2,64,1536]{2,1,0:T(8,128)(2,1)S(1)} %bitcast.38, bf16[2,1536,2048]{2,1,0:T(8,128)(2,1)} %param.11), kind=kOutput, calls=%fused_computation.7 | convolution fusion | flops 805568512 | bytes 13500416 | tf_op jit(solution)/shard_map/erd,edf->erf/dot_general | solution.py:46
  129.2 0.0 copy-start.3
  129.2 0.0 all-to-all-done
  129.2 3.4 %reshape.62 = bf16[6144,2,16]{2,1,0:T(2,128)(2,1)} reshape(bf16[4,2,24576]{2,1,0:T(2,128)(2,1)S(1)} %all-to-all-done) | data formatting | bytes 786432
  132.6 7.3 %copy.36 = bf16[2,16,4,1536]{3,2,1,0:T(4,128)(2,1)S(1)} copy(bf16[2,16,4,1536]{1,0,3,2:T(2,128)(2,1)} %bitcast.44) | data formatting | bytes 786432 | tf_op jit(solution)/shard_map/all_to_all | solution.py:40
  139.9 0.1 copy.29
  140.0 9.2 %convolution_convert_fusion.2 = bf16[2,64,2048]{2,1,0:T(8,128)(2,1)} fusion(bf16[2,64,1536]{2,1,0:T(8,128)(2,1)S(1)} %bitcast.45, bf16[2,2048,1536]{2,1,0:T(8,128)(2,1)} %param.12), kind=kOutput, calls=%fused_computation.8 | convolution fusion | flops 805568512 | bytes 13500416 | tf_op jit(solution)/shard_map/erd,efd->erf/dot_general | solution.py:47
  149.3 0.0 all-reduce.3.cloned.1.call-update
  149.3 0.0 copy-done.3
  149.3 5.7 %psum.31 = s32[2,1]{0,1:T(1,128)S(1)} all-reduce(s32[2,1]{0,1:T(1,128)S(1)} %copy-done.3), channel_id=1, replica_groups=mesh['dp'=4,'shard'=8] {'dp'}, use_global_device_ids=true, to_apply=%region_4.5 | all-reduce | flops 2 | bytes 16 | tf_op jit(solution)/shard_map/psum | solution.py:42
  155.0 38.9 %all-reduce.3.cloned.1.call-done = (bf16[2,64,2048]{2,1,0:T(8,128)(2,1)}, bf16[2,64,2048]{2,1,0:T(8,128)(2,1)}, bf16[2,64,2048]{2,1,0:T(8,128)(2,1)}) async-done(((bf16[2,64,2048]{2,1,0:T(8,128)(2,1)}, bf16[2,64,2048]{2,1,0:T(8,128)(2,1)}, bf16[2,64,2048]{2,1,0:T(8,128)(2,1)}), (bf16[2,64,2048]{2,1,0:T(8,128)(2,1)}, bf16[2,64,2048]{2,1,0:T(8,128)(2,1)}, ...) | async-done | bytes 1572880 | tf_op jit(solution)/shard_map/psum | solution.py:50
  193.9 0.0 copy-start.4
  193.9 0.0 copy-start.5
  193.9 9.1 %fusion.20 = f32[2,64,1536]{2,1,0:T(8,128)S(1)} fusion(bf16[2,1536,2048]{2,1,0:T(8,128)(2,1)} %param.10, bf16[2,64,2048]{2,1,0:T(8,128)(2,1)} %get-tuple-element.4, bf16[2,64,2048]{2,1,0:T(8,128)(2,1)} %get-tuple-element.5, bf16[2,64,2048]{2,1,0:T(8,128)(2,1)} %get-tuple-element.6), kind=kOutput, calls=%fused_computation.38 | convolution fusion | flops 808714240 | bytes 14942208 | tf_op jit(solution)/shard_map/erf,edf->erd/dot_general | solution.py:69
  203.0 0.0 copy-done.4
  203.0 0.0 copy-done.5
  203.0 0.0 copy-start.6
  203.0 8.6 %fusion = bf16[2,64,1536]{2,1,0:T(8,128)(2,1)S(1)} fusion(f32[2,64,1536]{2,1,0:T(8,128)S(1)} %fusion.20, bf16[2,1536,2048]{2,1,0:T(8,128)(2,1)} %param.11, bf16[2,64,2048]{2,1,0:T(8,128)(2,1)S(1)} %copy-done.5, bf16[2,64,2048]{2,1,0:T(8,128)(2,1)S(1)} %copy-done.4), kind=kOutput, calls=%fused_computation.9 | convolution fusion | flops 807796736 | bytes 14811136 | tf_op jit(solution)/shard_map/erf,edf->erd/dot_general | solution.py:70
  211.6 1.2 copy.33
  212.7 3.5 %all-to-all-start.2 = ((bf16[2,64,1536]{2,0,1:T(2,128)(2,1)}), bf16[2,64,1536]{2,0,1:T(2,128)(2,1)S(1)}, u32[]{:S(2)}, u32[]{:S(2)}) async-start(bf16[2,64,1536]{2,0,1:T(2,128)(2,1)} %copy.33), calls=%async_computation.2 | async-start | bytes 786432 | tf_op jit(solution)/shard_map/all_to_all | solution.py:72
  216.2 0.3 reduce-scatter.2.cloned.1.call-start
  216.4 0.0 copy-done.6
  216.5 6.7 %divide_convert_fusion.2 = bf16[2,1536,2048]{2,1,0:T(8,128)(2,1)} fusion(f32[2]{0:T(128)S(1)} %convert_bitcast_fusion, bf16[2,64,1536]{2,1,0:T(8,128)(2,1)S(1)} %bitcast.39, bf16[2,64,2048]{2,1,0:T(8,128)(2,1)S(1)} %copy-done.6, bf16[2,64,2048]{2,1,0:T(8,128)(2,1)S(1)} %copy-done.4, bf16[2,64,2048]{2,1,0:T(8,128)(2,1)S(1)} %copy-done.5), kind=kOutput, calls=%fused_computation.4 | convolution fusion | flops 821297152 | bytes 14549000 | tf_op jit(solution)/shard_map/erd,erf->edf/dot_general | solution.py:61
  223.2 6.9 %divide_convert_fusion = bf16[2,2048,1536]{2,1,0:T(8,128)(2,1)} fusion(f32[2]{0:T(128)S(1)} %convert_bitcast_fusion, bf16[2,64,1536]{2,1,0:T(8,128)(2,1)S(1)} %bitcast.46, bf16[2,64,2048]{2,1,0:T(8,128)(2,1)S(1)} %copy-done.6, bf16[2,64,2048]{2,1,0:T(8,128)(2,1)S(1)} %copy-done.5), kind=kOutput, calls=%fused_computation.2 | convolution fusion | flops 819986432 | bytes 14024712 | tf_op jit(solution)/shard_map/erf,erd->efd/dot_general | solution.py:57
  230.1 0.0 all-to-all-done.2
  230.1 0.3 copy.34
  230.4 1.0 all_to_all.50
  231.4 0.0 reduce-scatter.2.cloned.1.call-update
  231.4 0.0 copy-start.2
  231.4 0.0 copy-start.1
  231.5 6.7 %divide_convert_fusion.1 = bf16[2,1536,2048]{2,1,0:T(8,128)(2,1)} fusion(f32[2]{0:T(128)S(1)} %convert_bitcast_fusion, bf16[2,64,1536]{2,1,0:T(8,128)(2,1)S(1)} %bitcast.40, bf16[2,64,2048]{2,1,0:T(8,128)(2,1)S(1)} %copy-done.5, bf16[2,64,2048]{2,1,0:T(8,128)(2,1)S(1)} %copy-done.4), kind=kOutput, calls=%fused_computation.3 | convolution fusion | flops 819986432 | bytes 14024712 | tf_op jit(solution)/shard_map/erd,erf->edf/dot_general | solution.py:65
  238.2 56.8 %reduce-scatter.2.cloned.1.call-done = bf16[2,16,768]{2,1,0:T(8,128)(2,1)} async-done(((bf16[2,16,6144]{2,1,0:T(8,128)(2,1)}), bf16[2,16,768]{2,1,0:T(8,128)(2,1)}) %reduce-scatter.2.cloned.1.call-update) | async-done | bytes 49168 | tf_op jit(solution)/shard_map/reduce_scatter | solution.py:73
  295.0 0.0 copy-done.2
  295.0 1.7 fusion.1
  296.7 0.0 copy-done.1
  (2 shorter events, 0.0 us)
Async XLA Ops:
  7.2 0.9 copy-start
  51.9 47.7 %all-to-all-start.1 = ((bf16[4,2,24576]{2,1,0:T(2,128)(2,1)}), bf16[4,2,24576]{2,1,0:T(2,128)(2,1)S(1)}, u32[]{:S(2)}, u32[]{:S(2)}) async-start(bf16[4,2,24576]{2,1,0:T(2,128)(2,1)} %reshape.59), calls=%async_computation.1 | async-start | bytes 786432 | tf_op jit(solution)/shard_map/all_to_all | solution.py:39
  99.6 29.6 %all-to-all-start = ((bf16[4,2,24576]{2,1,0:T(2,128)(2,1)}), bf16[4,2,24576]{2,1,0:T(2,128)(2,1)S(1)}, u32[]{:S(2)}, u32[]{:S(2)}) async-start(bf16[4,2,24576]{2,1,0:T(2,128)(2,1)} %reshape.61), calls=%async_computation | async-start | bytes 786432 | tf_op jit(solution)/shard_map/all_to_all | solution.py:40
  103.1 90.8 %all-reduce.3.cloned.1.call-start = ((), (), s32[]{:S(2)}) async-start(), calls=%async_computation.5 | async-start | bytes 3145728 | tf_op jit(solution)/shard_map/psum | solution.py:50
  129.2 20.0 %copy-start.3 = (s32[2,1]{0,1:T(1,128)S(1)}, s32[2,1]{0,1:T(1,128)}, u32[]{:S(2)}) copy-start(s32[2,1]{0,1:T(1,128)} %param.15) | copy-start | bytes 28
  193.9 9.1 %copy-start.4 = (bf16[2,64,2048]{2,1,0:T(8,128)(2,1)S(1)}, bf16[2,64,2048]{2,1,0:T(8,128)(2,1)}, u32[]{:S(2)}) copy-start(bf16[2,64,2048]{2,1,0:T(8,128)(2,1)} %get-tuple-element.5) | copy-start | bytes 1572868
  193.9 9.1 %copy-start.5 = (bf16[2,64,2048]{2,1,0:T(8,128)(2,1)S(1)}, bf16[2,64,2048]{2,1,0:T(8,128)(2,1)}, u32[]{:S(2)}) copy-start(bf16[2,64,2048]{2,1,0:T(8,128)(2,1)} %get-tuple-element.6) | copy-start | bytes 1572868
  203.0 13.5 %copy-start.6 = (bf16[2,64,2048]{2,1,0:T(8,128)(2,1)S(1)}, bf16[2,64,2048]{2,1,0:T(8,128)(2,1)}, u32[]{:S(2)}) copy-start(bf16[2,64,2048]{2,1,0:T(8,128)(2,1)} %get-tuple-element.4) | copy-start | bytes 1572868
  212.7 17.4 %all-to-all-start.2 = ((bf16[2,64,1536]{2,0,1:T(2,128)(2,1)}), bf16[2,64,1536]{2,0,1:T(2,128)(2,1)S(1)}, u32[]{:S(2)}, u32[]{:S(2)}) async-start(bf16[2,64,1536]{2,0,1:T(2,128)(2,1)} %copy.33), calls=%async_computation.2 | async-start | bytes 786432 | tf_op jit(solution)/shard_map/all_to_all | solution.py:72
  216.2 78.8 %reduce-scatter.2.cloned.1.call-start = ((), (), s32[]{:S(2)}) async-start(), calls=%async_computation.4 | async-start | bytes 442368 | tf_op jit(solution)/shard_map/reduce_scatter | solution.py:73
  231.4 63.5 %copy-start.2 = (s32[2,16]{1,0:T(2,128)S(1)}, s32[2,16]{1,0:T(2,128)}, u32[]{:S(2)}) copy-start(s32[2,16]{1,0:T(2,128)} %param.13) | copy-start | bytes 388
  231.4 65.3 %copy-start.1 = (bf16[64,768]{1,0:T(8,128)(2,1)S(1)}, bf16[64,768]{1,0:T(8,128)(2,1)}, u32[]{:S(2)}) copy-start(bf16[64,768]{1,0:T(8,128)(2,1)} %param.8) | copy-start | bytes 294916
Sparse Core Ops, SparseCore 0:
  149.4 44.4 all-reduce.2
  231.6 63.3 reduce-scatter.1
